TPU v7x, 32 devices: a whole 2x2x4 slice. The times are simulated.
32 devices in a mesh: gx: 16 (over z, y, x), gy: 2 (over core).
Axes of the slice: x: 2, y: 2, z: 4, core: 2. Of those that a mesh axis runs over, the one named last changes fastest.
Arguments:
- observed: float32 [8192, 128], P(('gx', 'gy')), may hold values from -6 to 6
- jacobian: bfloat16 [8192, 64, 128], P(('gx', 'gy'))
- tile_block: int32 [8192], P(('gx', 'gy')), may hold values from 0 to 127
- params: float32 [128, 64], replicated, may hold values from -3 to 3
- damping: float32 [1], replicated, may hold values from 0.05 to 2
Outputs:
- scaled_step: float32 [128, 64], P('gy')
- misfit: float32 [], replicated
All inputs are finite; a program needn't handle non-finite values.
Results may differ from a plain program's by a relative error of at most 0.0031.
Values sent between devices are 32-bit elements; how exact they have to be, the bound alone decides.
No kernel may reach another device: no remote copies, remote signals or barrier semaphores. Data moves between devices by JAX's collectives and lax.ppermute only.
A program may use at most 64 MiB of HBM per device.

v0:
```python
import jax
import jax.numpy as jnp
from jax import lax
from jax.sharding import PartitionSpec as P

NB = 128


def swapped(value, axis, bit):
    return lax.ppermute(value, axis, [(i, i ^ 1 << bit) for i in range(lax.axis_size(axis))])


def solve_blocks(system, rhs):
    size = system.shape[1]
    augmented = jnp.concatenate([system, rhs[:, :, None]], axis=2)
    augmented = jnp.transpose(augmented, (1, 2, 0))
    row_ids = jnp.arange(size, dtype=jnp.int32)

    def eliminate(step, current):
        column = step.astype(jnp.int32)
        pivot_row = lax.dynamic_index_in_dim(current, column, 0, keepdims=False)
        pivot = lax.dynamic_index_in_dim(pivot_row, column, 0, keepdims=False)
        pivot_row = pivot_row / pivot[None, :]
        factors = lax.dynamic_index_in_dim(current, column, 1, keepdims=False)
        updated = current - factors[:, None, :] * pivot_row[None, :, :]
        is_pivot = (row_ids == column)[:, None, None]
        return jnp.where(is_pivot, pivot_row[None, :, :], updated)

    final = lax.fori_loop(0, size, eliminate, augmented)
    return jnp.transpose(final[:, size, :], (1, 0))


def local(observed, jacobian, tile_block, params, damping):
    moved = observed
    for bit_x in range(lax.axis_size("gx").bit_length() - 1):
        moved = swapped(moved, "gx", bit_x)
    for bit_y in range(lax.axis_size("gy").bit_length() - 1):
        moved = swapped(moved, "gy", bit_y)
    reflected_values = moved[::-1, ::-1]
    block_ids = jnp.arange(NB, dtype=jnp.int32)
    onehot = (tile_block[:, None] == block_ids[None, :]).astype(jnp.float32)
    tile_params = jnp.dot(onehot, params, precision=lax.Precision.HIGHEST).astype(jnp.bfloat16)
    calculated_values = jnp.einsum(
        "tpv,tp->tv", jacobian, tile_params, preferred_element_type=jnp.float32
    )
    residual_values = 0.5 * (observed + reflected_values) - calculated_values
    local_misfit = jnp.sum(residual_values * residual_values)
    resid_b = residual_values.astype(jnp.bfloat16)
    tile_grad = jnp.einsum("tpv,tv->tp", jacobian, resid_b, preferred_element_type=jnp.float32)
    tile_gram = jnp.einsum("tpv,tqv->tpq", jacobian, jacobian, preferred_element_type=jnp.float32)
    gram = jnp.einsum("tb,tpq->bpq", onehot, tile_gram, precision=lax.Precision.HIGHEST)
    grad = jnp.dot(onehot.T, tile_grad, precision=lax.Precision.HIGHEST)
    owned = NB // lax.axis_size("gy")
    gram, grad, total_misfit = lax.psum((gram, grad, local_misfit), ("gx", "gy"))
    leading_entry = lax.axis_index("gy") * owned
    gram = lax.dynamic_slice_in_dim(gram, leading_entry, owned, 0)
    grad = lax.dynamic_slice_in_dim(grad, leading_entry, owned, 0)
    misfit = total_misfit / (
        observed.shape[0] * lax.axis_size("gx") * lax.axis_size("gy") * observed.shape[1]
    )
    diagonal = jnp.diagonal(gram, axis1=1, axis2=2)
    eye = jnp.eye(gram.shape[1], dtype=jnp.float32)
    system = gram + damping[0] * diagonal[:, :, None] * eye[None] + eye[None]
    delta = solve_blocks(system, grad)
    return (delta * jnp.sqrt(diagonal), misfit)


def solution(mesh):
    return jax.shard_map(
        local,
        mesh=mesh,
        in_specs=(P(("gx", "gy"), None), P(("gx", "gy"), None, None), P(("gx", "gy")), P(), P()),
        out_specs=(P("gy", None), P()),
        check_vma=False,
    )
```

profile of v0, /device:TPU:0, one launch (start us, length us, event | category | flops | bytes accessed | tf_op | source)
XLA Modules:
  0.0 237.3 jit_solution(4161908257750440027)
XLA Ops:
  7.2 3.0 %collective-permute-start = (f32[256,128]{1,0:T(8,128)}, f32[256,128]{1,0:T(8,128)S(1)}, u32[]{:S(2)}, u32[]{:S(2)}) collective-permute-start(f32[256,128]{1,0:T(8,128)} %param.7), channel_id=1, source_target_pairs={{0,2},{2,0},{4,6},{6,4},{8,10},{10,8},{12,14},{14,12},{16,18},{18,... | collective-permute-start | bytes 393224 | tf_op jit(solution)/shard_map/ppermute | solution.py:10
  10.3 3.7 %collective-permute-done = f32[256,128]{1,0:T(8,128)S(1)} collective-permute-done((f32[256,128]{1,0:T(8,128)}, f32[256,128]{1,0:T(8,128)S(1)}, u32[]{:S(2)}, u32[]{:S(2)}) %collective-permute-start) | collective-permute-done | bytes 131104 | tf_op jit(solution)/shard_map/ppermute | solution.py:10
  14.0 1.8 collective-permute-start.1
  15.7 5.8 %fusion.21 = f32[256,64,64]{2,1,0:T(8,128)S(1)} fusion(bf16[256,64,128]{2,1,0:T(8,128)(2,1)} %param.8), kind=kOutput, calls=%fused_computation.37 | convolution fusion | flops 268435456 | bytes 8388608 | tf_op jit(solution)/shard_map/tpv,tqv->tpq/dot_general | solution.py:50
  21.5 1.6 collective-permute-start.2
  23.2 10.1 %fusion.3 = f32[128,64,64]{2,0,1:T(8,128)} fusion(f32[256,64,64]{2,1,0:T(8,128)S(1)} %fusion.21, s32[256]{0:T(256)S(1)} %copy-done.2), kind=kOutput, calls=%fused_computation.8 | convolution fusion | flops 1610645504 | bytes 6292480 | tf_op jit(solution)/shard_map/tb,tpq->bpq/dot_general | solution.py:51
  33.6 2.7 %collective-permute-start.3 = (f32[256,128]{1,0:T(8,128)S(1)}, f32[256,128]{1,0:T(8,128)S(1)}, u32[]{:S(2)}, u32[]{:S(2)}) collective-permute-start(f32[256,128]{1,0:T(8,128)S(1)} %collective-permute-done.2), channel_id=1, source_target_pairs={{0,16},{2,18},{4,20},{6,22},{8,24},{10,26},{12,28},{14,30},{16,0},... | collective-permute-start | bytes 393224 | tf_op jit(solution)/shard_map/ppermute | solution.py:10
  36.2 3.7 %fusion.8 = f32[256,1,128]{2,1,0:T(1,128)S(1)} fusion(bf16[256,64,128]{2,1,0:T(8,128)(2,1)} %param.8, bf16[256,64,1]{1,0,2:T(8,128)(2,1)S(1)} %fusion.5), kind=kOutput, calls=%fused_computation.16 | convolution fusion | flops 4194304 | bytes 4358144 | tf_op jit(solution)/shard_map/tpv,tp->tv/dot_general | solution.py:43
  39.9 1.3 collective-permute-done.3
  41.8 0.7 collective-permute-done.4
  42.7 0.6 multiply_reduce_fusion
  43.3 4.6 %fusion.6 = f32[256,1,64]{2,1,0:T(1,128)S(1)} fusion(bf16[256,64,128]{2,1,0:T(8,128)(2,1)} %param.8, bf16[256,128,1]{1,0,2:T(8,128)(2,1)S(1)} %get-tuple-element.124), kind=kOutput, calls=%fused_computation.14 | convolution fusion | flops 4194304 | bytes 4325376 | tf_op jit(solution)/shard_map/tpv,tv->tp/dot_general | solution.py:49
  48.1 40.2 %all-reduce = (f32[128,64]{1,0:T(8,128)S(1)}, f32[]{:T(128)}) all-reduce(f32[128,64]{1,0:T(8,128)S(1)} %fusion.10, f32[]{:T(128)} %get-tuple-element.123), channel_id=1, replica_groups=mesh['gx'=16,'gy'=2] {'gx','gy'}, use_global_device_ids=true, to_apply=%region_1.0 | all-reduce | flops 8193 | bytes 65544 | tf_op jit(solution)/shard_map/psum | solution.py:54
  88.3 1.9 copy.13
  90.9 84.2 %all-reduce.3.cloned.1.call-done = f32[128,64,64]{2,0,1:T(8,128)} async-done(((f32[128,64,64]{2,0,1:T(8,128)}), f32[128,64,64]{2,0,1:T(8,128)}) %all-reduce.3.cloned.1.call-update) | async-done | bytes 2097168 | tf_op jit(solution)/shard_map/psum | solution.py:54
  175.2 3.2 %constant_dynamic-slice_fusion.2 = f32[64,64,64]{2,0,1:T(8,128)} fusion(f32[128,64,64]{2,0,1:T(8,128)} %all-reduce.3.cloned.1.call-done, s32[]{:T(128)S(6)} %select_n.46), kind=kLoop, calls=%fused_computation.36 | loop fusion | bytes 2097156 | tf_op jit(solution)/shard_map/dynamic_slice | solution.py:56
  178.4 2.9 %copy.12 = f32[64,64,64]{0,2,1:T(8,128)} copy(f32[64,64,64]{2,0,1:T(8,128)} %constant_dynamic-slice_fusion.2) | data formatting | bytes 2097152 | tf_op jit(solution)/shard_map/dynamic_slice | solution.py:56
  181.3 1.5 gather_fusion
  182.8 2.0 add_add_fusion
  184.7 2.0 maximum_bitcast_fusion
  186.7 2.2 copy.14
  188.9 39.3 %while.17 = (s32[]{:T(128)}, f32[64,65,64]{2,1,0:T(8,128)S(1)}, s32[]{:T(128)}, s32[]{:T(128)}, s32[]{:T(128)}, /*index=5*/s32[]{:T(128)}) while((s32[]{:T(128)}, f32[64,65,64]{2,1,0:T(8,128)S(1)}, s32[]{:T(128)}, s32[]{:T(128)}, s32[]{:T(128)}, /*index=5*/s32[]{:T(128)}) %tuple.51), condition=%wide.region_3.0_spmd.clone, body=%wide.region_2.0_spmd.clone.sunk | while | flops 802948 | bytes 2230009 | solution.py:29
  189.6 0.5 subtract_select_fusion.2
  190.8 0.5 subtract_select_fusion.2
  192.1 0.5 subtract_select_fusion.2
  193.3 0.5 subtract_select_fusion.2
  194.5 0.5 subtract_select_fusion.2
  195.7 0.5 subtract_select_fusion.2
  197.0 0.5 subtract_select_fusion.2
  200.0 0.5 subtract_select_fusion.2
  201.3 0.5 subtract_select_fusion.2
  228.6 0.7 copy.16
  (331 shorter events, 32.7 us)
Async XLA Ops:
  7.2 26.1 %copy-start = (f32[128,64]{0,1:T(8,128)S(1)}, f32[128,64]{0,1:T(8,128)}, u32[]{:S(2)}) copy-start(f32[128,64]{0,1:T(8,128)} %param.10) | copy-start | bytes 98308
  7.2 16.0 %copy-start.2 = (s32[256]{0:T(256)S(1)}, s32[256]{0:T(256)}, u32[]{:S(2)}) copy-start(s32[256]{0:T(256)} %param.9) | copy-start | bytes 3076
  7.2 168.0 %all-reduce.3.cloned.1.call-start = ((), (), s32[]{:S(2)}) async-start(), calls=%async_computation | async-start | bytes 8388608 | tf_op jit(solution)/shard_map/psum | solution.py:54
  7.2 6.7 %collective-permute-start = (f32[256,128]{1,0:T(8,128)}, f32[256,128]{1,0:T(8,128)S(1)}, u32[]{:S(2)}, u32[]{:S(2)}) collective-permute-start(f32[256,128]{1,0:T(8,128)} %param.7), channel_id=1, source_target_pairs={{0,2},{2,0},{4,6},{6,4},{8,10},{10,8},{12,14},{14,12},{16,18},{18,... | collective-permute-start | bytes 393224 | tf_op jit(solution)/shard_map/ppermute | solution.py:10
  14.0 7.5 %collective-permute-start.1 = (f32[256,128]{1,0:T(8,128)S(1)}, f32[256,128]{1,0:T(8,128)S(1)}, u32[]{:S(2)}, u32[]{:S(2)}) collective-permute-start(f32[256,128]{1,0:T(8,128)S(1)} %collective-permute-done), channel_id=1, source_target_pairs={{0,4},{2,6},{4,0},{6,2},{8,12},{10,14},{12,8},{14,10},{16,20},{18,... | collective-permute-start | bytes 393224 | tf_op jit(solution)/shard_map/ppermute | solution.py:10
  21.5 12.0 %collective-permute-start.2 = (f32[256,128]{1,0:T(8,128)S(1)}, f32[256,128]{1,0:T(8,128)S(1)}, u32[]{:S(2)}, u32[]{:S(2)}) collective-permute-start(f32[256,128]{1,0:T(8,128)S(1)} %collective-permute-done.1), channel_id=1, source_target_pairs={{0,8},{2,10},{4,12},{6,14},{8,0},{10,2},{12,4},{14,6},{16,24},{18,... | collective-permute-start | bytes 393224 | tf_op jit(solution)/shard_map/ppermute | solution.py:10
  33.6 9.1 %copy-start.1 = (f32[256,128]{1,0:T(8,128)S(1)}, f32[256,128]{1,0:T(8,128)}, u32[]{:S(2)}) copy-start(f32[256,128]{1,0:T(8,128)} %param.7) | copy-start | bytes 393220
  33.6 7.6 %collective-permute-start.3 = (f32[256,128]{1,0:T(8,128)S(1)}, f32[256,128]{1,0:T(8,128)S(1)}, u32[]{:S(2)}, u32[]{:S(2)}) collective-permute-start(f32[256,128]{1,0:T(8,128)S(1)} %collective-permute-done.2), channel_id=1, source_target_pairs={{0,16},{2,18},{4,20},{6,22},{8,24},{10,26},{12,28},{14,30},{16,0},... | collective-permute-start | bytes 393224 | tf_op jit(solution)/shard_map/ppermute | solution.py:10
  41.2 1.3 collective-permute-start.4
Sparse Core Ops, SparseCore 0:
  33.4 141.7 all-reduce.2
where the time goes:
time: 238 us; the launch traced here: 237 us
  waiting for transfers between devices  89.9 us (38%)
  blocking collectives  40.2 us (17%)
  other arithmetic  37.7 us (16%)
  matrix products  24.6 us (10%)
  between operations  16.6 us (7%)
  local copies, waits for them, and re-layouts  15.8 us (7%)
  starting transfers between devices  9.14 us (4%)
  loops' own time  3.37 us (1%)
    psum x1, waiting for transfers between devices, local(): lax.psum((gram, grad, local_misfit), ('gx', 'gy'))  84.2 us
    psum x1, blocking collectives, local(): lax.psum((gram, grad, local_misfit), ('gx', 'gy'))  40.2 us
    select_n x64, other arithmetic, eliminate(): return jnp.where(is_pivot, pivot_row[None, :, :], updated)  31.8 us
    dot_general x1, matrix products, local(): jnp.einsum('tb,tpq->bpq', onehot, tile_gram, precision=lax.Precision.HIGH...  10.1 us
    ppermute x5, starting transfers between devices, swapped(): lax.ppermute(value, axis, [(i, i ^ 1 << bit) for i in range(lax.axis_size...  9.1 us
    dynamic_slice x2, local copies, waits for them, and re-layouts, local(): gram = lax.dynamic_slice_in_dim(gram, leading_entry, owned, 0)  6.08 us
    dot_general x1, matrix products, local(): jnp.einsum('tpv,tqv->tpq', jacobian, jacobian, preferred_element_type=jnp...  5.77 us
    ppermute x5, waiting for transfers between devices, swapped(): lax.ppermute(value, axis, [(i, i ^ 1 << bit) for i in range(lax.axis_size...  5.65 us
  transfers between devices with their start and end apart: 6, of which 4 were waited for; matrix products, arithmetic and copies ran while one was open for 12% of the time, Pallas kernels for 0%

commit v1 on v0

--- a/solution.py
+++ b/solution.py
@@ -51,7 +51,7 @@
     gram = jnp.einsum("tb,tpq->bpq", onehot, tile_gram, precision=lax.Precision.HIGHEST)
     grad = jnp.dot(onehot.T, tile_grad, precision=lax.Precision.HIGHEST)
     owned = NB // lax.axis_size("gy")
-    gram, grad, total_misfit = lax.psum((gram, grad, local_misfit), ("gx", "gy"))
+    gram, grad, total_misfit = lax.psum(lax.psum((gram, grad, local_misfit), "gy"), "gx")
     leading_entry = lax.axis_index("gy") * owned
     gram = lax.dynamic_slice_in_dim(gram, leading_entry, owned, 0)
     grad = lax.dynamic_slice_in_dim(grad, leading_entry, owned, 0)

time: 238 us -> 298 us (1.25)
  blocking collectives: 40.2 us -> 84 us
  waiting for transfers between devices: 89.9 us -> 108 us
    psum x1 -> x2, blocking collectives: 40.2 us -> 84 us  [the longest x1 79.3 us: local(): lax.psum(lax.psum((gram, grad, local_misfit), 'gy'), 'gx')]
    ppermute x5, waiting for transfers between devices: 5.65 us -> 26.1 us  [swapped(): lax.ppermute(value, axis, [(i, i ^ 1 << bit) for i in range(lax.axis_size...]
    psum x1 -> x2, waiting for transfers between devices: 84.2 us -> 82.1 us  [the longest x1 51.4 us: local(): lax.psum(lax.psum((gram, grad, local_misfit), 'gy'), 'gx')]
  transfers between devices with their start and end apart: 6 -> 7, of which waited for: 4 -> 7; matrix products, arithmetic and copies ran while one was open for 12% -> 4% of each run, Pallas kernels for 0% -> 0%
where the time goes in v1:
time: 298 us
  waiting for transfers between devices  108 us (36%)
  blocking collectives  84 us (28%)
  other arithmetic  37.7 us (13%)
  matrix products  24.2 us (8%)
  between operations  16.6 us (6%)
  local copies, waits for them, and re-layouts  15.8 us (5%)
  starting transfers between devices  7.76 us (3%)
  loops' own time  3.37 us (1%)
    psum x1, blocking collectives, local(): lax.psum(lax.psum((gram, grad, local_misfit), 'gy'), 'gx')  79.3 us
    psum x1, waiting for transfers between devices, local(): lax.psum(lax.psum((gram, grad, local_misfit), 'gy'), 'gx')  51.4 us
    select_n x64, other arithmetic, eliminate(): return jnp.where(is_pivot, pivot_row[None, :, :], updated)  31.8 us
    psum x1, waiting for transfers between devices, local(): lax.psum((gram, grad, local_misfit), 'gy')  30.7 us
    ppermute x5, waiting for transfers between devices, swapped(): lax.ppermute(value, axis, [(i, i ^ 1 << bit) for i in range(lax.axis_size...  26.1 us
    dot_general x1, matrix products, local(): jnp.einsum('tb,tpq->bpq', onehot, tile_gram, precision=lax.Precision.HIGH...  10 us
    ppermute x5, starting transfers between devices, swapped(): lax.ppermute(value, axis, [(i, i ^ 1 << bit) for i in range(lax.axis_size...  7.5 us
    dynamic_slice x2, local copies, waits for them, and re-layouts, local(): gram = lax.dynamic_slice_in_dim(gram, leading_entry, owned, 0)  6.07 us
  transfers between devices with their start and end apart: 7, of which 7 were waited for; matrix products, arithmetic and copies ran while one was open for 4% of the time, Pallas kernels for 0%

profile of v1, /device:TPU:0, one launch (start us, length us, event | category | flops | bytes accessed | tf_op | source)
XLA Modules:
  0.0 297.6 jit_solution(11901290467826480776)
XLA Ops:
  7.2 5.8 %fusion.21 = f32[256,64,64]{2,1,0:T(8,128)S(1)} fusion(bf16[256,64,128]{2,1,0:T(8,128)(2,1)} %param.8), kind=kOutput, calls=%fused_computation.37 | convolution fusion | flops 268435456 | bytes 8388608 | tf_op jit(solution)/shard_map/tpv,tqv->tpq/dot_general | solution.py:50
  13.0 10.0 %fusion.3 = f32[128,64,64]{2,0,1:T(8,128)} fusion(f32[256,64,64]{2,1,0:T(8,128)S(1)} %fusion.21, s32[256]{0:T(256)S(1)} %copy-done.2), kind=kOutput, calls=%fused_computation.8 | convolution fusion | flops 1610645504 | bytes 6292480 | tf_op jit(solution)/shard_map/tb,tpq->bpq/dot_general | solution.py:51
  23.3 30.7 %all-reduce.5.cloned.1.call-done = f32[128,64,64]{2,0,1:T(8,128)} async-done(((f32[128,64,64]{2,0,1:T(8,128)}), f32[128,64,64]{2,0,1:T(8,128)}) %all-reduce.5.cloned.1.call-update) | async-done | bytes 2097168 | tf_op jit(solution)/shard_map/psum | solution.py:54
  54.1 1.8 collective-permute-start
  55.9 3.9 %collective-permute-done = f32[256,128]{1,0:T(8,128)S(1)} collective-permute-done((f32[256,128]{1,0:T(8,128)S(1)}, f32[256,128]{1,0:T(8,128)S(1)}, u32[]{:S(2)}, u32[]{:S(2)}) %collective-permute-start) | collective-permute-done | bytes 131104 | tf_op jit(solution)/shard_map/ppermute | solution.py:10
  59.8 1.7 collective-permute-start.1
  61.6 3.2 %collective-permute-done.1 = f32[256,128]{1,0:T(8,128)S(1)} collective-permute-done((f32[256,128]{1,0:T(8,128)S(1)}, f32[256,128]{1,0:T(8,128)S(1)}, u32[]{:S(2)}, u32[]{:S(2)}) %collective-permute-start.1) | collective-permute-done | bytes 131104 | tf_op jit(solution)/shard_map/ppermute | solution.py:10
  64.8 1.8 collective-permute-start.2
  66.8 9.3 %collective-permute-done.2 = f32[256,128]{1,0:T(8,128)S(1)} collective-permute-done((f32[256,128]{1,0:T(8,128)S(1)}, f32[256,128]{1,0:T(8,128)S(1)}, u32[]{:S(2)}, u32[]{:S(2)}) %collective-permute-start.2) | collective-permute-done | bytes 131104 | tf_op jit(solution)/shard_map/ppermute | solution.py:10
  76.1 2.2 collective-permute-start.3
  78.3 3.4 %fusion.8 = f32[256,1,128]{2,1,0:T(1,128)S(1)} fusion(bf16[256,64,128]{2,1,0:T(8,128)(2,1)} %param.8, bf16[256,64,1]{1,0,2:T(8,128)(2,1)S(1)} %fusion.5), kind=kOutput, calls=%fused_computation.16 | convolution fusion | flops 4194304 | bytes 4358144 | tf_op jit(solution)/shard_map/tpv,tp->tv/dot_general | solution.py:43
  81.7 9.0 %collective-permute-done.3 = f32[256,128]{1,0:T(8,128)S(1)} collective-permute-done((f32[256,128]{1,0:T(8,128)S(1)}, f32[256,128]{1,0:T(8,128)S(1)}, u32[]{:S(2)}, u32[]{:S(2)}) %collective-permute-start.3) | collective-permute-done | bytes 131104 | tf_op jit(solution)/shard_map/ppermute | solution.py:10
  91.4 0.7 collective-permute-done.4
  92.2 0.7 multiply_reduce_fusion
  92.9 4.5 %fusion.6 = f32[256,1,64]{2,1,0:T(1,128)S(1)} fusion(bf16[256,64,128]{2,1,0:T(8,128)(2,1)} %param.8, bf16[256,128,1]{1,0,2:T(8,128)(2,1)S(1)} %get-tuple-element.126), kind=kOutput, calls=%fused_computation.14 | convolution fusion | flops 4194304 | bytes 4325376 | tf_op jit(solution)/shard_map/tpv,tv->tp/dot_general | solution.py:49
  97.6 4.7 %all-reduce.1 = (f32[128,64]{1,0:T(8,128)S(1)}, f32[]{:T(128)}) all-reduce(f32[128,64]{1,0:T(8,128)S(1)} %fusion.10, f32[]{:T(128)} %get-tuple-element.125), channel_id=1, replica_groups=mesh['gx'=16,'gy'=2] {'gy'}, use_global_device_ids=true, to_apply=%region_2.0 | all-reduce | flops 8193 | bytes 65544 | tf_op jit(solution)/shard_map/psum | solution.py:54
  102.3 79.3 %all-reduce = (f32[128,64]{1,0:T(8,128)S(1)}, f32[]{:T(128)}) all-reduce(f32[128,64]{1,0:T(8,128)S(1)} %get-tuple-element.123, f32[]{:T(128)} %get-tuple-element.124), channel_id=1, replica_groups=mesh['gx'=16,'gy'=2] {'gx'}, use_global_device_ids=true, to_apply=%region_3.0 | all-reduce | flops 8193 | bytes 65544 | tf_op jit(solution)/shard_map/psum | solution.py:54
  181.6 1.9 copy.13
  184.2 51.4 %all-reduce.7.cloned.1.call-done = f32[128,64,64]{2,0,1:T(8,128)} async-done(((f32[128,64,64]{2,0,1:T(8,128)}), f32[128,64,64]{2,0,1:T(8,128)}) %all-reduce.7.cloned.1.call-update) | async-done | bytes 2097168 | tf_op jit(solution)/shard_map/psum | solution.py:54
  235.5 3.2 %constant_dynamic-slice_fusion.2 = f32[64,64,64]{2,0,1:T(8,128)} fusion(f32[128,64,64]{2,0,1:T(8,128)} %all-reduce.7.cloned.1.call-done, s32[]{:T(128)S(6)} %select_n.46), kind=kLoop, calls=%fused_computation.36 | loop fusion | bytes 2097156 | tf_op jit(solution)/shard_map/dynamic_slice | solution.py:56
  238.7 2.9 copy.12
  241.6 1.5 gather_fusion
  243.1 2.0 add_add_fusion
  245.1 2.0 maximum_bitcast_fusion
  247.0 2.2 copy.14
  249.2 39.3 %while.17 = (s32[]{:T(128)}, f32[64,65,64]{2,1,0:T(8,128)S(1)}, s32[]{:T(128)}, s32[]{:T(128)}, s32[]{:T(128)}, /*index=5*/s32[]{:T(128)}) while((s32[]{:T(128)}, f32[64,65,64]{2,1,0:T(8,128)S(1)}, s32[]{:T(128)}, s32[]{:T(128)}, s32[]{:T(128)}, /*index=5*/s32[]{:T(128)}) %tuple.51), condition=%wide.region_5.0_spmd.clone, body=%wide.region_4.0_spmd.clone.sunk | while | flops 802948 | bytes 2230009 | solution.py:29
  249.9 0.5 subtract_select_fusion.2
  251.2 0.5 subtract_select_fusion.2
  252.4 0.5 subtract_select_fusion.2
  253.6 0.5 subtract_select_fusion.2
  254.8 0.5 subtract_select_fusion.2
  289.0 0.7 copy.16
  (335 shorter events, 34.9 us)
Async XLA Ops:
  7.2 59.4 %copy-start = (f32[128,64]{0,1:T(8,128)S(1)}, f32[128,64]{0,1:T(8,128)}, u32[]{:S(2)}) copy-start(f32[128,64]{0,1:T(8,128)} %param.10) | copy-start | bytes 98308
  7.2 5.8 %copy-start.2 = (s32[256]{0:T(256)S(1)}, s32[256]{0:T(256)}, u32[]{:S(2)}) copy-start(s32[256]{0:T(256)} %param.9) | copy-start | bytes 3076
  7.2 46.9 %all-reduce.5.cloned.1.call-start = ((), (), s32[]{:S(2)}) async-start(), calls=%async_computation | async-start | bytes 8388608 | tf_op jit(solution)/shard_map/psum | solution.py:54
  23.1 31.0 %copy-start.1 = (f32[256,128]{1,0:T(8,128)S(1)}, f32[256,128]{1,0:T(8,128)}, u32[]{:S(2)}) copy-start(f32[256,128]{1,0:T(8,128)} %param.7) | copy-start | bytes 393220
  23.1 212.4 %all-reduce.7.cloned.1.call-start = ((), (), s32[]{:S(2)}) async-start(), calls=%async_computation.1 | async-start | bytes 8388608 | tf_op jit(solution)/shard_map/psum | solution.py:54
  54.1 5.8 %collective-permute-start = (f32[256,128]{1,0:T(8,128)S(1)}, f32[256,128]{1,0:T(8,128)S(1)}, u32[]{:S(2)}, u32[]{:S(2)}) collective-permute-start(f32[256,128]{1,0:T(8,128)S(1)} %copy-done.1), channel_id=1, source_target_pairs={{0,2},{2,0},{4,6},{6,4},{8,10},{10,8},{12,14},{14,12},{16,18},{18,... | collective-permute-start | bytes 393224 | tf_op jit(solution)/shard_map/ppermute | solution.py:10
  59.8 5.0 %collective-permute-start.1 = (f32[256,128]{1,0:T(8,128)S(1)}, f32[256,128]{1,0:T(8,128)S(1)}, u32[]{:S(2)}, u32[]{:S(2)}) collective-permute-start(f32[256,128]{1,0:T(8,128)S(1)} %collective-permute-done), channel_id=1, source_target_pairs={{0,4},{2,6},{4,0},{6,2},{8,12},{10,14},{12,8},{14,10},{16,20},{18,... | collective-permute-start | bytes 393224 | tf_op jit(solution)/shard_map/ppermute | solution.py:10
  64.8 11.3 %collective-permute-start.2 = (f32[256,128]{1,0:T(8,128)S(1)}, f32[256,128]{1,0:T(8,128)S(1)}, u32[]{:S(2)}, u32[]{:S(2)}) collective-permute-start(f32[256,128]{1,0:T(8,128)S(1)} %collective-permute-done.1), channel_id=1, source_target_pairs={{0,8},{2,10},{4,12},{6,14},{8,0},{10,2},{12,4},{14,6},{16,24},{18,... | collective-permute-start | bytes 393224 | tf_op jit(solution)/shard_map/ppermute | solution.py:10
  76.1 14.6 %collective-permute-start.3 = (f32[256,128]{1,0:T(8,128)S(1)}, f32[256,128]{1,0:T(8,128)S(1)}, u32[]{:S(2)}, u32[]{:S(2)}) collective-permute-start(f32[256,128]{1,0:T(8,128)S(1)} %collective-permute-done.2), channel_id=1, source_target_pairs={{0,16},{2,18},{4,20},{6,22},{8,24},{10,26},{12,28},{14,30},{16,0},... | collective-permute-start | bytes 393224 | tf_op jit(solution)/shard_map/ppermute | solution.py:10
  90.7 1.3 collective-permute-start.4
Sparse Core Ops, SparseCore 0:
  23.2 30.7 all-reduce.4
  59.7 175.7 all-reduce.6
